TPU v7x, 512 devices: a whole 4x8x8 slice. The times are simulated.
512 devices in a mesh: dp: 32 (over y, z_hi), seq: 16 (over x, z_lo, core).
Axes of the slice: x: 4, y: 8, z: 8 (z_hi: 4, z_lo: 2; z = z_hi * 2 + z_lo), core: 2. Of those that a mesh axis runs over, the one named last changes fastest.
Arguments:
- queries: bfloat16 [32, 2048, 2048], P('dp', 'seq'), may hold values from -6 to 6
- grad_out: bfloat16 [32, 2048, 2048], P('dp', 'seq'), may hold values from -6 to 6
- encoded: bfloat16 [32, 32, 64, 896], P('dp', 'seq'), may hold values from -6 to 6
- kv_weight: bfloat16 [896, 4096], P(None, 'dp'), may hold values from -0.1875 to 0.1875
- neighbour_ids: int32 [32, 32, 2], P('dp', 'seq'), may hold values from 0 to 31, all different within a row
- slot_map: int32 [32, 32], P('dp'), may hold values from 0 to 31, each once within a row
Outputs:
- attended: bfloat16 [32, 2048, 2048], P('dp', 'seq')
- grad_queries: bfloat16 [32, 2048, 2048], P('dp', 'seq')
- grad_encoded: float32 [32, 32, 64, 896], P('dp', 'seq')
Inputs may be any that keep to these rules, and one draw needn't show every extreme that they name: `neighbour_ids`: each span names 2 different neighbour ids of its own sequence. `slot_map`: for each sequence a permutation; storage position p lies on the seq index p // 2.
All inputs are finite; a program needn't handle non-finite values.
Results may differ from a plain program's by a relative error of at most 0.018.
Values may be sent and summed in bfloat16 or wider, within the bound.
A program may use at most 64 MiB of HBM per device.

v0:
```python
import jax
import jax.numpy as jnp
from jax import lax
from jax.sharding import PartitionSpec as P

HEAD_SIZE = 128
HEADS = 16
SPAN = 64
NLEN = 64
READS = 2


def lookup_positions(neighbour_ids, slot_map):
    pool_size = slot_map.shape[1]
    matches = neighbour_ids[0][:, :, None] == jnp.arange(pool_size, dtype=jnp.int32)[None, None, :]
    positions = jnp.sum(jnp.where(matches, slot_map[0][None, None, :], 0), axis=2)
    return positions.reshape(-1)


def per_device(queries, grad_out, encoded, kv_weight, neighbour_ids, slot_map):
    hidden = HEADS * HEAD_SIZE
    scale_factor = HEAD_SIZE ** (-0.5)
    spans = queries.shape[1] // SPAN
    pool_size = slot_map.shape[1]
    width_enc = encoded.shape[3]
    flat_pos = lookup_positions(neighbour_ids, slot_map)
    read_count = flat_pos.shape[0]
    read_rows = read_count * NLEN
    pool_rows = lax.all_gather(encoded, "seq", axis=1, tiled=True)[0]
    picked = jnp.take(pool_rows, flat_pos, axis=0).reshape(read_rows, width_enc)
    whole_weight = lax.all_gather(kv_weight, "dp", axis=1, tiled=True)
    kv_flat = jnp.dot(picked, whole_weight, preferred_element_type=jnp.float32).astype(jnp.bfloat16)
    kv_spans = kv_flat.reshape(spans, READS * NLEN, 2 * hidden)
    keys = kv_spans[:, :, :hidden].reshape(spans, READS * NLEN, HEADS, HEAD_SIZE)
    values = kv_spans[:, :, hidden:].reshape(spans, READS * NLEN, HEADS, HEAD_SIZE)
    query_tiles = queries[0].reshape(spans, SPAN, HEADS, HEAD_SIZE)
    grad_tiles = grad_out[0].reshape(spans, SPAN, HEADS, HEAD_SIZE)
    scores = (
        jnp.einsum("cqhd,ckhd->chqk", query_tiles, keys, preferred_element_type=jnp.float32)
        * scale_factor
    )
    expos = jnp.exp(scores)
    probs = expos / jnp.sum(expos, axis=-1, keepdims=True)
    probs_low = probs.astype(jnp.bfloat16)
    attended = jnp.einsum("chqk,ckhd->cqhd", probs_low, values, preferred_element_type=jnp.float32)
    attended = attended.astype(jnp.bfloat16).reshape(1, spans * SPAN, hidden)
    d_probs = jnp.einsum("cqhd,ckhd->chqk", grad_tiles, values, preferred_element_type=jnp.float32)
    delta = jnp.sum(probs * d_probs, axis=-1, keepdims=True)
    d_scores = (probs * (d_probs - delta) * scale_factor).astype(jnp.bfloat16)
    grad_queries = jnp.einsum("chqk,ckhd->cqhd", d_scores, keys, preferred_element_type=jnp.float32)
    grad_queries = grad_queries.astype(jnp.bfloat16).reshape(1, spans * SPAN, hidden)
    d_keys = jnp.einsum(
        "chqk,cqhd->ckhd", d_scores, query_tiles, preferred_element_type=jnp.float32
    )
    d_values = jnp.einsum(
        "chqk,cqhd->ckhd", probs_low, grad_tiles, preferred_element_type=jnp.float32
    )
    grad_reads = jnp.concatenate(
        [d_keys.reshape(read_rows, hidden), d_values.reshape(read_rows, hidden)], axis=-1
    ).astype(jnp.bfloat16)
    enc_reads = lax.dot_general(
        grad_reads, whole_weight, (((1,), (1,)), ((), ())), preferred_element_type=jnp.float32
    )
    enc_reads = enc_reads.reshape(read_count, NLEN, width_enc)
    onehot = (flat_pos[:, None] == jnp.arange(pool_size, dtype=jnp.int32)[None, :]).astype(
        jnp.float32
    )
    partial_value = jnp.einsum("rn,rlk->nlk", onehot, enc_reads, precision=lax.Precision.HIGHEST)
    rounded = lax.optimization_barrier(partial_value.astype(jnp.bfloat16))
    grad_encoded = lax.psum_scatter(
        rounded.astype(jnp.float32)[None].astype(jnp.bfloat16),
        "seq",
        scatter_dimension=1,
        tiled=True,
    ).astype(jnp.float32)
    return (attended, grad_queries, grad_encoded)


def solution(mesh):
    in_specs = (
        P("dp", "seq", None),
        P("dp", "seq", None),
        P("dp", "seq", None, None),
        P(None, "dp"),
        P("dp", "seq", None),
        P("dp", None),
    )
    out_specs = (P("dp", "seq", None), P("dp", "seq", None), P("dp", "seq", None, None))
    return jax.shard_map(
        per_device, mesh=mesh, in_specs=in_specs, out_specs=out_specs, check_vma=False
    )
```

profile of v0, /device:TPU:16, one launch (start us, length us, event | category | flops | bytes accessed | tf_op | source)
XLA Modules:
  0.0 315.2 jit_solution(13738438806581832548)
XLA Ops:
  9.9 1.2 copy.73
  11.1 1.1 copy.74
  12.3 44.6 %all-gather.3.cloned.1.call-done = bf16[1,32,64,896]{3,2,0,1:T(8,128)(2,1)} async-done(((bf16[1,2,64,896]{3,2,0,1:T(8,128)(2,1)}), bf16[1,32,64,896]{3,2,0,1:T(8,128)(2,1)}) %all-gather.3.cloned.1.call-update) | async-done | bytes 3670032 | tf_op jit(solution)/shard_map/all_gather | solution.py:29
  56.8 2.7 gather_fusion
  59.6 140.9 %all-gather.5.cloned.1.call-done = bf16[896,4096]{1,0:T(8,128)(2,1)} async-done(((bf16[896,128]{1,0:T(8,128)(2,1)}), bf16[896,4096]{1,0:T(8,128)(2,1)}) %all-gather.5.cloned.1.call-update) | async-done | bytes 7340048 | tf_op jit(solution)/shard_map/all_gather | solution.py:31
  200.5 5.4 %convolution_convert_fusion = bf16[256,4096]{1,0:T(8,128)(2,1)S(1)} fusion(bf16[256,896]{1,0:T(8,128)(2,1)S(1)} %bitcast_select_fusion, bf16[896,4096]{1,0:T(8,128)(2,1)} %all-gather.5.cloned.1.call-done), kind=kOutput, calls=%fused_computation.2 | convolution fusion | flops 1880096768 | bytes 9895936 | tf_op jit(solution)/shard_map/dot_general | solution.py:32
  206.0 1.3 fusion.42
  207.9 2.0 copy.72
  210.3 1.1 copy-done.2
  211.4 1.3 fusion.23
  212.7 3.5 %fusion.6 = bf16[2,128,16,128]{3,1,2,0:T(8,128)(2,1)} fusion(bf16[2,64,16,128]{3,2,1,0:T(8,128)(2,1)S(1)} %bitcast.70, f32[2,16,64,128]{3,2,1,0:T(8,128)} %copy-done.2), kind=kOutput, calls=%fused_computation.11 | convolution fusion | flops 68159616 | bytes 2621440 | tf_op jit(solution)/shard_map/chqk,cqhd->ckhd/dot_general | solution.py:55
  216.2 1.4 convolution_bitcast_fusion
  217.6 3.0 copy.63
  220.6 2.9 fusion.5
  224.2 1.7 copy_bitcast_fusion
  225.9 5.7 %fusion.1 = f32[256,896]{1,0:T(8,128)S(1)} fusion(bf16[896,4096]{1,0:T(8,128)(2,1)} %all-gather.5.cloned.1.call-done, bf16[256,2048]{1,0:T(8,128)(2,1)S(1)} %get-tuple-element.17, bf16[256,2048]{1,0:T(8,128)(2,1)S(1)} %get-tuple-element.18), kind=kOutput, calls=%fused_computation.4 | convolution fusion | flops 1883242496 | bytes 10354688 | tf_op jit(solution)/shard_map/dot_general | solution.py:61
  231.6 3.8 %convolution_convert_fusion.1 = bf16[32,64,896]{2,0,1:T(8,128)(2,1)S(1)} fusion(f32[4,64,896]{2,1,0:T(8,128)S(1)} %bitcast.73, s32[4]{0:T(128)S(1)} %reshape.80), kind=kOutput, calls=%fused_computation.3 | convolution fusion | flops 89915520 | bytes 4587536 | tf_op jit(solution)/shard_map/rn,rlk->nlk/dot_general | solution.py:68
  235.4 3.1 copy.65
  238.5 1.2 copy-done.1
  239.7 2.6 fusion.13
  242.6 1.0 reshape.85
  243.6 3.0 fusion.14
  248.0 58.8 %reduce-scatter.2.cloned.1.call-done = bf16[1,2,64,896]{3,2,0,1:T(8,128)(2,1)} async-done(((bf16[1,32,64,896]{3,2,0,1:T(8,128)(2,1)}), bf16[1,2,64,896]{3,2,0,1:T(8,128)(2,1)}) %reduce-scatter.2.cloned.1.call-update) | async-done | bytes 229392 | tf_op jit(solution)/shard_map/reduce_scatter | solution.py:70
  306.9 1.7 bitcast_convert_fusion
  (25 shorter events, 6.4 us)
Async XLA Ops:
  7.2 49.7 %all-gather.3.cloned.1.call-start = ((), (), s32[]{:S(2)}) async-start(), calls=%async_computation.1 | async-start | bytes 3899392 | tf_op jit(solution)/shard_map/all_gather | solution.py:29
  7.9 192.7 %all-gather.5.cloned.1.call-start = ((), (), s32[]{:S(2)}) async-start(), calls=%async_computation.2 | async-start | bytes 7569408 | tf_op jit(solution)/shard_map/all_gather | solution.py:31
  8.6 298.2 %reduce-scatter.2.cloned.1.call-start = ((), (), s32[]{:S(2)}) async-start(), calls=%async_computation.3 | async-start | bytes 3899392 | tf_op jit(solution)/shard_map/reduce_scatter | solution.py:70
  207.9 8.3 %copy-start = (bf16[2,128,2048]{1,2,0:T(8,128)(2,1)}, bf16[2,128,2048]{1,2,0:T(8,128)(2,1)S(1)}, u32[]{:S(2)}) copy-start(bf16[2,128,2048]{1,2,0:T(8,128)(2,1)S(1)} %copy.71) | copy-start | bytes 3145732
  210.3 1.1 copy-start.2
  238.5 1.2 copy-start.1
Sparse Core Ops, SparseCore 0:
  10.1 46.6 all-gather.2
  59.9 140.6 all-gather.4
  238.6 68.2 reduce-scatter.1
where the time goes:
time: 316 us; the launch traced here: 315 us
  waiting for transfers between devices  246 us (78%)
  matrix products  28.7 us (9%)
  local copies, waits for them, and re-layouts  22.6 us (7%)
  between operations  13.9 us (4%)
  other arithmetic  4.12 us (1%)
    all_gather x1, waiting for transfers between devices, per_device(): whole_weight = lax.all_gather(kv_weight, 'dp', axis=1, tiled=True)  141 us
    reduce_scatter x1, waiting for transfers between devices, per_device(): lax.psum_scatter(rounded.astype(jnp.float32)[None].astype(jnp.bfloat16),...  58.8 us
    all_gather x1, waiting for transfers between devices, per_device(): pool_rows = lax.all_gather(encoded, 'seq', axis=1, tiled=True)[0]  44.6 us
    unnamed x10, local copies, waits for them, and re-layouts  7.21 us
  transfers between devices with their start and end apart: 3, of which 3 were waited for; matrix products, arithmetic and copies ran while one was open for 5% of the time, Pallas kernels for 0%

commit v1 on v0

--- a/solution.py
+++ b/solution.py
@@ -28,7 +28,9 @@
     read_rows = read_count * NLEN
     pool_rows = lax.all_gather(encoded, "seq", axis=1, tiled=True)[0]
     picked = jnp.take(pool_rows, flat_pos, axis=0).reshape(read_rows, width_enc)
-    whole_weight = lax.all_gather(kv_weight, "dp", axis=1, tiled=True)
+    whole_weight = jnp.concatenate(
+        lax.all_to_all(jnp.stack([kv_weight] * lax.axis_size("dp")), "dp", 0, 0), axis=1
+    )
     kv_flat = jnp.dot(picked, whole_weight, preferred_element_type=jnp.float32).astype(jnp.bfloat16)
     kv_spans = kv_flat.reshape(spans, READS * NLEN, 2 * hidden)
     keys = kv_spans[:, :, :hidden].reshape(spans, READS * NLEN, HEADS, HEAD_SIZE)

time: 316 us -> 388 us (1.23)
  the two profiles are of different devices: /device:TPU:16 before, /device:TPU:8 now
where the time goes in v1:
time: 388 us
  waiting for transfers between devices  298 us (77%)
  matrix products  28.8 us (7%)
  local copies, waits for them, and re-layouts  26.6 us (7%)
  starting transfers between devices  16.4 us (4%)
  between operations  14.2 us (4%)
    all_gather x1, waiting for transfers between devices, per_device(): pool_rows = lax.all_gather(encoded, 'seq', axis=1, tiled=True)[0]  214 us
    reduce_scatter x1, waiting for transfers between devices, per_device(): lax.psum_scatter(rounded.astype(jnp.float32)[None].astype(jnp.bfloat16),...  83.5 us
    all_to_all x1, starting transfers between devices, per_device(): lax.all_to_all(jnp.stack([kv_weight] * lax.axis_size('dp')), 'dp', 0, 0)  16.4 us
  transfers between devices with their start and end apart: 3, of which 2 were waited for; matrix products, arithmetic and copies ran while one was open for 3% of the time, Pallas kernels for 0%

profile of v1, /device:TPU:8, one launch (start us, length us, event | category | flops | bytes accessed | tf_op | source)
XLA Modules:
  0.0 387.8 jit_solution(10796559772806150468)
XLA Ops:
  7.2 1.1 copy.51
  8.3 4.1 %stack.2 = bf16[32,896,128]{1,2,0:T(8,128)(2,1)} broadcast(bf16[896,128]{0,1:T(8,128)(2,1)S(1)} %copy.51), dimensions={1,2} | broadcast | bytes 7569408 | tf_op jit(solution)/shard_map/stack | solution.py:32
  12.3 16.4 %all-to-all-start = ((bf16[32,896,128]{1,2,0:T(8,128)(2,1)}), bf16[32,896,128]{1,2,0:T(8,128)(2,1)}, u32[]{:S(2)}, u32[]{:S(2)}) async-start(bf16[32,896,128]{1,2,0:T(8,128)(2,1)} %stack.2), calls=%async_computation | async-start | bytes 14680064 | tf_op jit(solution)/shard_map/all_to_all | solution.py:32
  30.2 214.0 %all-gather.2.cloned.1.call-done = bf16[1,32,64,896]{3,2,0,1:T(8,128)(2,1)} async-done(((bf16[1,2,64,896]{3,2,0,1:T(8,128)(2,1)}), bf16[1,32,64,896]{3,2,0,1:T(8,128)(2,1)}) %all-gather.2.cloned.1.call-update) | async-done | bytes 3670032 | tf_op jit(solution)/shard_map/all_gather | solution.py:29
  244.2 2.7 gather_fusion
  247.0 5.4 %convolution_convert_fusion = bf16[256,4096]{1,0:T(8,128)(2,1)S(1)} fusion(bf16[256,896]{1,0:T(8,128)(2,1)S(1)} %bitcast.72, bf16[896,4096]{0,1:T(8,128)(2,1)} %bitcast.7), kind=kOutput, calls=%fused_computation.2 | convolution fusion | flops 1880096768 | bytes 9895936 | tf_op jit(solution)/shard_map/dot_general | solution.py:34
  252.5 1.3 fusion.42
  254.4 2.0 copy.77
  257.9 1.3 fusion.23
  259.2 3.5 fusion.6
  262.7 1.4 convolution_bitcast_fusion
  264.1 1.9 copy.65
  266.0 1.3 concatenate.10
  267.3 2.9 fusion.5
  270.2 1.7 copy.63
  272.0 1.5 concatenate.9
  273.5 5.8 %fusion.1 = f32[4,64,896]{2,1,0:T(8,128)S(1)} fusion(bf16[896,4096,1]{0,1,2:T(8,128)(2,1)} %bitcast.19, bf16[4,64,2048]{2,1,0:T(8,128)(2,1)} %concatenate.10, bf16[4,64,2048]{2,1,0:T(8,128)(2,1)S(1)} %concatenate.9), kind=kOutput, calls=%fused_computation.4 | convolution fusion | flops 1883242496 | bytes 10354688 | tf_op jit(solution)/shard_map/dot_general | solution.py:63
  279.2 3.8 convolution_convert_fusion.1
  283.0 3.1 copy.68
  286.1 1.2 copy-done.1
  287.3 2.6 fusion.13
  291.3 3.0 fusion.14
  295.7 83.5 %reduce-scatter.2.cloned.1.call-done = bf16[1,2,64,896]{3,2,0,1:T(8,128)(2,1)} async-done(((bf16[1,32,64,896]{3,2,0,1:T(8,128)(2,1)}), bf16[1,2,64,896]{3,2,0,1:T(8,128)(2,1)}) %reduce-scatter.2.cloned.1.call-update) | async-done | bytes 229392 | tf_op jit(solution)/shard_map/reduce_scatter | solution.py:72
  379.2 1.7 bitcast_convert_fusion
  (33 shorter events, 6.4 us)
Async XLA Ops:
  12.3 17.2 %copy-start.5 = (s32[1,2,2]{2,1,0:T(2,128)S(1)}, s32[1,2,2]{2,1,0:T(2,128)}, u32[]{:S(2)}) copy-start(s32[1,2,2]{2,1,0:T(2,128)} %param.10) | copy-start | bytes 52
  12.3 17.2 %copy-start.6 = (s32[1,32]{1,0:T(1,128)S(1)}, s32[1,32]{1,0:T(1,128)}, u32[]{:S(2)}) copy-start(s32[1,32]{1,0:T(1,128)} %param.11) | copy-start | bytes 388
  12.3 17.6 %copy-start.3 = (bf16[1,128,2048]{2,1,0:T(8,128)(2,1)S(1)}, bf16[1,128,2048]{2,1,0:T(8,128)(2,1)}, u32[]{:S(2)}) copy-start(bf16[1,128,2048]{2,1,0:T(8,128)(2,1)} %param.6) | copy-start | bytes 1572868
  12.3 17.7 %copy-start.4 = (bf16[1,128,2048]{2,1,0:T(8,128)(2,1)S(1)}, bf16[1,128,2048]{2,1,0:T(8,128)(2,1)}, u32[]{:S(2)}) copy-start(bf16[1,128,2048]{2,1,0:T(8,128)(2,1)} %param.7) | copy-start | bytes 1572868
  12.3 234.6 %all-to-all-start = ((bf16[32,896,128]{1,2,0:T(8,128)(2,1)}), bf16[32,896,128]{1,2,0:T(8,128)(2,1)}, u32[]{:S(2)}, u32[]{:S(2)}) async-start(bf16[32,896,128]{1,2,0:T(8,128)(2,1)} %stack.2), calls=%async_computation | async-start | bytes 14680064 | tf_op jit(solution)/shard_map/all_to_all | solution.py:32
  28.7 215.5 %all-gather.2.cloned.1.call-start = ((), (), s32[]{:S(2)}) async-start(), calls=%async_computation.2 | async-start | bytes 3899392 | tf_op jit(solution)/shard_map/all_gather | solution.py:29
  29.5 349.7 %reduce-scatter.2.cloned.1.call-start = ((), (), s32[]{:S(2)}) async-start(), calls=%async_computation.3 | async-start | bytes 3899392 | tf_op jit(solution)/shard_map/reduce_scatter | solution.py:72
  254.4 8.3 %copy-start = (bf16[2,128,2048]{1,2,0:T(8,128)(2,1)}, bf16[2,128,2048]{1,2,0:T(8,128)(2,1)S(1)}, u32[]{:S(2)}) copy-start(bf16[2,128,2048]{1,2,0:T(8,128)(2,1)S(1)} %copy.76) | copy-start | bytes 3145732
  256.8 1.1 copy-start.2
  286.1 1.2 copy-start.1
Sparse Core Ops, SparseCore 0:
  31.7 212.4 all-gather.1
  286.2 92.9 reduce-scatter.1
